TPU v7x, 512 devices: a whole 4x8x8 slice. The times are simulated.
512 devices in a mesh: dp: 32 (over x, y), table: 16 (over z, core).
Axes of the slice: x: 4, y: 8, z: 8, core: 2. Of those that a mesh axis runs over, the one named last changes fastest.
Arguments:
- table: bfloat16 [12288, 512], P('table'), may hold values from -6 to 6
- history_shard: int32 [512, 256, 1], P(('dp', 'table')), may hold values from 0 to 15; in each aligned block of 256 rows (0 to 255, 256 to 511, ..., all dimensions but the last counted through in order) at most 32 rows name the same one
- history_row: int32 [512, 256], P(('dp', 'table')), may hold values from 0 to 767
- lengths: int32 [512], P(('dp', 'table')), may hold values from 1 to 256, 98304 in all
- w_in: bfloat16 [512, 2048], replicated, may hold values from -0.25 to 0.25
- w_out: bfloat16 [512, 512], replicated, may hold values from -0.25 to 0.25
- cotangent: bfloat16 [512, 256, 512], P(('dp', 'table')), may hold values from -6 to 6
Outputs:
- table_grad: float32 [12288, 512], P('table')
- dense_grad: bfloat16 [512, 512], replicated
Inputs may be any that keep to these rules, and one draw needn't show every extreme that they name: `history_shard`: among the 256 history slots of one device's samples, at most 32 name one table shard, and that bound is met by some shard in some device's slots. `lengths`: some sample has the full length 256.
All inputs are finite; a program needn't handle non-finite values. No bound on the sum of `lengths` on one device may be relied on, other than what follows from the above.
Results may differ from a plain program's by a relative error of at most 0.017.
Values may be sent and summed in bfloat16 or wider, within the bound.
A program may use at most 64 MiB of HBM per device.

v0:
```python
import math
import jax
import jax.numpy as jnp
from jax import lax
from jax.sharding import PartitionSpec as P

HEADS = 4


def layer_norm(values):
    average = jnp.mean(values, axis=-1, keepdims=True)
    centred = values - average
    variance = jnp.mean(centred * centred, axis=-1, keepdims=True)
    return centred * lax.rsqrt(variance + 1e-06)


def hstu_layer(embedded, w_in, w_out, lengths):
    samples_here, seq_span, model_width = embedded.shape
    head_dim = model_width // HEADS
    normed = layer_norm(embedded.astype(jnp.float32)).astype(jnp.bfloat16)
    projected = jax.nn.silu(
        jnp.dot(
            normed.reshape(samples_here * seq_span, model_width),
            w_in,
            preferred_element_type=jnp.float32,
        )
    )
    gate_part = projected[:, :model_width]
    shaped = (samples_here, seq_span, HEADS, head_dim)
    values = projected[:, model_width : 2 * model_width].astype(jnp.bfloat16).reshape(shaped)
    queries = projected[:, 2 * model_width : 3 * model_width].astype(jnp.bfloat16).reshape(shaped)
    keys = projected[:, 3 * model_width :].astype(jnp.bfloat16).reshape(shaped)
    scores = jnp.einsum(
        "blhd,bmhd->bhlm", queries.astype(jnp.float32), keys.astype(jnp.float32)
    ) * head_dim ** (-0.5)
    positions = jnp.arange(seq_span)
    live_keys = (positions[None, None, :] <= positions[None, :, None]) & (
        positions[None, None, :] < lengths[:, None, None]
    )
    weights = (
        jnp.where(live_keys[:, None], jax.nn.silu(scores), 0.0)
        / lengths.astype(jnp.float32)[:, None, None, None]
    )
    weights = weights.astype(jnp.bfloat16)
    attended = jnp.einsum(
        "bhlm,bmhd->blhd", weights.astype(jnp.float32), values.astype(jnp.float32)
    ).reshape(samples_here * seq_span, model_width)
    mixed = (layer_norm(attended) * gate_part).astype(jnp.bfloat16)
    output = jnp.dot(mixed, w_out, preferred_element_type=jnp.float32) + embedded.reshape(
        -1, model_width
    ).astype(jnp.float32)
    return (output, mixed)


def per_device(table, history_shard, history_row, lengths, w_in, w_out, cotangent):
    shard_rows, model_width = table.shape
    samples_here, seq_span = history_row.shape
    groups = lax.axis_size("table")
    slot_count = samples_here * seq_span
    capacity = 2 * slot_count // groups
    owners = history_shard[:, :, 0].reshape(-1)
    local_rows = history_row.reshape(-1)
    owner_hits = (owners[:, None] == jnp.arange(groups)[None, :]).astype(jnp.int32)
    slot_rank = jnp.sum((jnp.cumsum(owner_hits, axis=0) - owner_hits) * owner_hits, axis=1)
    position = owners * capacity + slot_rank
    requested = (
        jnp.zeros((groups * capacity,), jnp.int32)
        .at[position]
        .set(local_rows)
        .reshape(groups, capacity)
    )
    incoming = lax.all_to_all(requested, "table", split_axis=0, concat_axis=0, tiled=True).reshape(
        -1
    )
    global_rows = owners * shard_rows + local_rows
    piece = lax.all_gather(table, "table", axis=0, tiled=True)
    inside = (global_rows >= 0) & (global_rows < piece.shape[0])
    taken = piece[jnp.clip(global_rows, 0, piece.shape[0] - 1)].astype(jnp.float32)
    embedded = jnp.where(inside[:, None], taken, 0.0).astype(jnp.bfloat16)
    embedded = embedded.reshape(samples_here, seq_span, model_width)
    output, pullback, mixed = jax.vjp(
        lambda rows_in: hstu_layer(rows_in, w_in, w_out, lengths), embedded, has_aux=True
    )
    row_live = jnp.arange(seq_span)[None, :] < lengths[:, None]
    grad_seed = jnp.where(row_live[:, :, None], cotangent, jnp.zeros_like(cotangent))
    flat_seed = grad_seed.reshape(-1, model_width)
    (row_grad,) = pullback(flat_seed.astype(jnp.float32))
    dense_part = jnp.dot(mixed.T, flat_seed, preferred_element_type=jnp.float32)
    outgoing = (
        jnp.zeros((groups * capacity, model_width), jnp.bfloat16)
        .at[position]
        .set(row_grad.reshape(-1, model_width))
    )
    arrived = lax.all_to_all(
        outgoing.reshape(groups, capacity, model_width),
        "table",
        split_axis=0,
        concat_axis=0,
        tiled=True,
    )
    local_grad = (
        jnp.zeros((shard_rows, model_width), jnp.float32)
        .at[incoming]
        .add(arrived.reshape(-1, model_width).astype(jnp.float32))
    )
    total_slots = slot_count * lax.axis_size("dp") * groups
    grad_scale = 1.0 / math.sqrt(total_slots)
    table_grad = lax.psum(local_grad, "dp")
    dense_total = lax.psum(dense_part, ("dp", "table"))
    dense_grad = (dense_total * grad_scale).astype(jnp.bfloat16)
    return (table_grad, dense_grad)


def solution(mesh):
    in_specs = (
        P("table", None),
        P(("dp", "table"), None, None),
        P(("dp", "table"), None),
        P(("dp", "table")),
        P(),
        P(),
        P(("dp", "table"), None, None),
    )
    out_specs = (P("table", None), P())
    return jax.shard_map(
        per_device, mesh=mesh, in_specs=in_specs, out_specs=out_specs, check_vma=False
    )
```

profile of v0, /device:TPU:64, one launch (start us, length us, event | category | flops | bytes accessed | tf_op | source)
XLA Modules:
  0.0 582.9 jit_solution(10138484838293075610)
XLA Ops:
  10.9 1.6 scatter_custom_fusion
  13.1 10.0 %all-to-all-start = ((s32[16,1,32]{2,1,0:T(1,128)}), s32[16,1,32]{2,1,0:T(1,128)S(1)}, u32[]{:S(2)}, u32[]{:S(2)}) async-start(s32[16,1,32]{2,1,0:T(1,128)} %all_to_all.9), calls=%async_computation | async-start | bytes 16384 | tf_op jit(solution)/shard_map/all_to_all | solution.py:72
  24.5 66.3 %all-gather.2.cloned.1.call-done = bf16[12288,512]{1,0:T(8,128)(2,1)} async-done(((bf16[768,512]{1,0:T(8,128)(2,1)}), bf16[12288,512]{1,0:T(8,128)(2,1)}) %all-gather.2.cloned.1.call-update) | async-done | bytes 12582928 | tf_op jit(solution)/shard_map/all_gather | solution.py:76
  90.8 7.4 %gather_fusion = bf16[256,512]{1,0:T(8,128)(2,1)S(1)} fusion(bf16[12288,512]{1,0:T(8,128)(2,1)} %all-gather.2.cloned.1.call-done, s32[1024]{0:T(1024)S(1)} %pad_clamp_fusion), kind=kCustom, calls=%fused_computation | custom fusion | bytes 525312 | tf_op jit(solution)/shard_map/gather | solution.py:78
  98.7 2.8 fusion.76
  102.5 1.6 divide_convert_fusion
  105.1 1.7 multiply_reduce_fusion.1
  106.9 2.1 fusion.75
  109.2 2.0 fusion.26
  111.5 1.0 fusion.79
  112.5 0.9 fusion.81
  113.6 1.8 copy.38
  115.4 1.8 copy.39
  117.2 3.4 multiply_reduce_fusion
  120.6 1.0 fusion.74
  121.6 2.9 scatter_custom_fusion.1
  124.5 6.9 %all-to-all-start.1 = ((bf16[16,32,512]{2,1,0:T(8,128)(2,1)}), bf16[16,32,512]{2,1,0:T(8,128)(2,1)}, u32[]{:S(2)}, u32[]{:S(2)}) async-start(bf16[16,32,512]{2,1,0:T(8,128)(2,1)} %bitcast.120), calls=%async_computation.1 | async-start | bytes 1048576 | tf_op jit(solution)/shard_map/all_to_all | solution.py:94
  131.6 2.5 fusion.45
  135.4 10.4 %all-to-all-done.1 = bf16[16,32,512]{2,1,0:T(8,128)(2,1)} async-done(((bf16[16,32,512]{2,1,0:T(8,128)(2,1)}), bf16[16,32,512]{2,1,0:T(8,128)(2,1)}, u32[]{:S(2)}, u32[]{:S(2)}) %all-to-all-start.1) | async-done | bytes 524320 | tf_op jit(solution)/shard_map/all_to_all | solution.py:94
  145.8 5.5 scatter_custom_fusion.2
  151.3 258.6 %all-reduce.9.cloned.1.call-done = f32[512,512]{1,0:T(8,128)} async-done(((f32[512,512]{1,0:T(8,128)}), f32[512,512]{1,0:T(8,128)}) %all-reduce.9.cloned.1.call-update) | async-done | bytes 1048592 | tf_op jit(solution)/shard_map/psum | solution.py:109
  409.9 2.1 multiply_convert_fusion
  412.0 161.6 %all-reduce.7.cloned.1.call-done = f32[768,512]{1,0:T(8,128)} async-done(((f32[768,512]{1,0:T(8,128)}), f32[768,512]{1,0:T(8,128)}) %all-reduce.7.cloned.1.call-update) | async-done | bytes 1572880 | tf_op jit(solution)/shard_map/psum | solution.py:108
  573.7 2.7 copy.58
  (60 shorter events, 9.8 us)
Async XLA Ops:
  7.2 91.5 %copy-start = (bf16[512,2048]{1,0:T(8,128)(2,1)S(1)}, bf16[512,2048]{1,0:T(8,128)(2,1)}, u32[]{:S(2)}) copy-start(bf16[512,2048]{1,0:T(8,128)(2,1)} %param.11) | copy-start | bytes 6291460
  7.2 83.6 %all-gather.2.cloned.1.call-start = ((), (), s32[]{:S(2)}) async-start(), calls=%async_computation.2 | async-start | bytes 13369344 | tf_op jit(solution)/shard_map/all_gather | solution.py:76
  13.1 111.4 %all-to-all-start = ((s32[16,1,32]{2,1,0:T(1,128)}), s32[16,1,32]{2,1,0:T(1,128)S(1)}, u32[]{:S(2)}, u32[]{:S(2)}) async-start(s32[16,1,32]{2,1,0:T(1,128)} %all_to_all.9), calls=%async_computation | async-start | bytes 16384 | tf_op jit(solution)/shard_map/all_to_all | solution.py:72
  102.4 1.8 copy-start.4
  102.5 1.6 copy-start.6
  102.5 1.6 copy-start.8
  104.1 0.8 copy-start.2
  109.2 2.1 copy-start.5
  109.2 2.3 copy-start.7
  111.2 1.3 copy-start.3
  117.2 4.4 copy-start.1
  124.5 21.3 %all-to-all-start.1 = ((bf16[16,32,512]{2,1,0:T(8,128)(2,1)}), bf16[16,32,512]{2,1,0:T(8,128)(2,1)}, u32[]{:S(2)}, u32[]{:S(2)}) async-start(bf16[16,32,512]{2,1,0:T(8,128)(2,1)} %bitcast.120), calls=%async_computation.1 | async-start | bytes 1048576 | tf_op jit(solution)/shard_map/all_to_all | solution.py:94
  131.4 278.5 %all-reduce.9.cloned.1.call-start = ((), (), s32[]{:S(2)}) async-start(), calls=%async_computation.4 | async-start | bytes 2097152 | tf_op jit(solution)/shard_map/psum | solution.py:109
  134.1 439.6 %all-reduce.7.cloned.1.call-start = ((), (), s32[]{:S(2)}) async-start(), calls=%async_computation.3 | async-start | bytes 3145728 | tf_op jit(solution)/shard_map/psum | solution.py:108
Sparse Core Ops, SparseCore 0:
  10.1 80.5 all-gather.1
  137.3 272.5 all-reduce.8
  414.3 159.3 all-reduce.6
where the time goes:
time: 584 us; the launch traced here: 583 us
  waiting for transfers between devices  498 us (85%)
  local copies, waits for them, and re-layouts  18.5 us (3%)
  other arithmetic  18.5 us (3%)
  starting transfers between devices  17.1 us (3%)
  matrix products  16.5 us (3%)
  between operations  14.6 us (2%)
    psum x1, waiting for transfers between devices, per_device(): dense_total = lax.psum(dense_part, ('dp', 'table'))  259 us
    psum x1, waiting for transfers between devices, per_device(): table_grad = lax.psum(local_grad, 'dp')  162 us
    all_gather x1, waiting for transfers between devices, per_device(): piece = lax.all_gather(table, 'table', axis=0, tiled=True)  66.3 us
  transfers between devices with their start and end apart: 5, of which 4 were waited for; matrix products, arithmetic and copies ran while one was open for 9% of the time, Pallas kernels for 0%

commit v1 on v0

--- a/solution.py
+++ b/solution.py
@@ -106,7 +106,7 @@
     total_slots = slot_count * lax.axis_size("dp") * groups
     grad_scale = 1.0 / math.sqrt(total_slots)
     table_grad = lax.psum(local_grad, "dp")
-    dense_total = lax.psum(dense_part, ("dp", "table"))
+    dense_total = lax.psum(lax.psum(dense_part, "dp"), "table")
     dense_grad = (dense_total * grad_scale).astype(jnp.bfloat16)
     return (table_grad, dense_grad)
 

time: 584 us -> 448 us (0.77)
  the two profiles are of different devices: /device:TPU:64 before, /device:TPU:1 now
where the time goes in v1:
time: 448 us; the launch traced here: 447 us
  waiting for transfers between devices  364 us (81%)
  other arithmetic  18.6 us (4%)
  local copies, waits for them, and re-layouts  17 us (4%)
  matrix products  16.5 us (4%)
  starting transfers between devices  16.4 us (4%)
  between operations  14.6 us (3%)
    psum x1, waiting for transfers between devices, per_device(): table_grad = lax.psum(local_grad, 'dp')  159 us
    psum x1, waiting for transfers between devices, per_device(): dense_total = lax.psum(lax.psum(dense_part, 'dp'), 'table')  121 us
    all_gather x1, waiting for transfers between devices, per_device(): piece = lax.all_gather(table, 'table', axis=0, tiled=True)  68.8 us
    all_to_all x1, waiting for transfers between devices, per_device(): lax.all_to_all(outgoing.reshape(groups, capacity, model_width), 'table',...  13.4 us
    all_to_all x1, starting transfers between devices, per_device(): lax.all_to_all(requested, 'table', split_axis=0, concat_axis=0, tiled=True)  11.8 us
  transfers between devices with their start and end apart: 5, of which 4 were waited for; matrix products, arithmetic and copies ran while one was open for 9% of the time, Pallas kernels for 0%

profile of v1, /device:TPU:1, one launch (start us, length us, event | category | flops | bytes accessed | tf_op | source)
XLA Modules:
  0.0 446.8 jit_solution(6523637485365780998)
XLA Ops:
  10.9 1.6 scatter_custom_fusion
  13.1 11.8 %all-to-all-start = ((s32[16,1,32]{2,1,0:T(1,128)}), s32[16,1,32]{2,1,0:T(1,128)S(1)}, u32[]{:S(2)}, u32[]{:S(2)}) async-start(s32[16,1,32]{2,1,0:T(1,128)} %all_to_all.9), calls=%async_computation | async-start | bytes 16384 | tf_op jit(solution)/shard_map/all_to_all | solution.py:72
  26.4 68.8 %all-gather.2.cloned.1.call-done = bf16[12288,512]{1,0:T(8,128)(2,1)} async-done(((bf16[768,512]{1,0:T(8,128)(2,1)}), bf16[12288,512]{1,0:T(8,128)(2,1)}) %all-gather.2.cloned.1.call-update) | async-done | bytes 12582928 | tf_op jit(solution)/shard_map/all_gather | solution.py:76
  95.2 7.4 %gather_fusion = bf16[256,512]{1,0:T(8,128)(2,1)S(1)} fusion(bf16[12288,512]{1,0:T(8,128)(2,1)} %all-gather.2.cloned.1.call-done, s32[1024]{0:T(1024)S(1)} %pad_clamp_fusion), kind=kCustom, calls=%fused_computation | custom fusion | bytes 525312 | tf_op jit(solution)/shard_map/gather | solution.py:78
  103.1 2.8 fusion.76
  107.0 1.6 divide_convert_fusion
  109.5 1.7 multiply_reduce_fusion.1
  111.3 2.1 fusion.75
  113.6 2.0 fusion.26
  115.9 1.0 fusion.79
  116.9 0.9 fusion.81
  118.0 1.8 copy.38
  119.8 1.8 copy.39
  121.6 3.4 multiply_reduce_fusion
  125.0 1.0 fusion.74
  126.0 2.9 scatter_custom_fusion.1
  128.9 4.3 all-to-all-start.1
  134.7 2.5 fusion.45
  137.2 13.4 %all-to-all-done.1 = bf16[16,32,512]{2,1,0:T(8,128)(2,1)} async-done(((bf16[16,32,512]{2,1,0:T(8,128)(2,1)}), bf16[16,32,512]{2,1,0:T(8,128)(2,1)}, u32[]{:S(2)}, u32[]{:S(2)}) %all-to-all-start.1) | async-done | bytes 524320 | tf_op jit(solution)/shard_map/all_to_all | solution.py:94
  150.6 5.4 %scatter_custom_fusion.2 = f32[768,512]{1,0:T(8,128)} fusion(s32[512]{0:T(512)S(1)} %bitcast.137, bf16[512,512]{1,0:T(8,128)(2,1)} %bitcast.42, f32[]{:T(128)} %constant.15.clone.1), kind=kCustom, calls=%fused_computation.35 | custom fusion | flops 524288 | bytes 2097156 | tf_op jit(solution)/shard_map/scatter-add | solution.py:104
  156.2 159.3 %all-reduce.10.cloned.1.call-done = (f32[768,512]{1,0:T(8,128)}, f32[512,512]{1,0:T(8,128)}) async-done(((f32[768,512]{1,0:T(8,128)}, f32[512,512]{1,0:T(8,128)}), (f32[768,512]{1,0:T(8,128)}, f32[512,512]{1,0:T(8,128)})) %all-reduce.10.cloned.1.call-update) | async-done | bytes 2621456 | tf_op jit(solution)/shard_map/psum | solution.py:108
  315.5 121.4 %all-reduce.8.cloned.1.call-done = f32[512,512]{1,0:T(8,128)} async-done(((f32[512,512]{1,0:T(8,128)}), f32[512,512]{1,0:T(8,128)}) %all-reduce.8.cloned.1.call-update) | async-done | bytes 1048592 | tf_op jit(solution)/shard_map/psum | solution.py:109
  436.9 2.3 multiply_convert_fusion
  439.1 1.1 copy.59
  (62 shorter events, 9.8 us)
Async XLA Ops:
  7.2 95.9 %copy-start = (bf16[512,2048]{1,0:T(8,128)(2,1)S(1)}, bf16[512,2048]{1,0:T(8,128)(2,1)}, u32[]{:S(2)}) copy-start(bf16[512,2048]{1,0:T(8,128)(2,1)} %param.11) | copy-start | bytes 6291460
  7.2 88.0 %all-gather.2.cloned.1.call-start = ((), (), s32[]{:S(2)}) async-start(), calls=%async_computation.2 | async-start | bytes 13369344 | tf_op jit(solution)/shard_map/all_gather | solution.py:76
  13.1 115.8 %all-to-all-start = ((s32[16,1,32]{2,1,0:T(1,128)}), s32[16,1,32]{2,1,0:T(1,128)S(1)}, u32[]{:S(2)}, u32[]{:S(2)}) async-start(s32[16,1,32]{2,1,0:T(1,128)} %all_to_all.9), calls=%async_computation | async-start | bytes 16384 | tf_op jit(solution)/shard_map/all_to_all | solution.py:72
  106.8 1.8 copy-start.5
  106.9 1.6 copy-start.7
  106.9 1.6 copy-start.9
  108.5 0.8 copy-start.2
  113.6 2.1 copy-start.6
  113.6 2.3 copy-start.8
  115.6 1.3 copy-start.3
  121.6 4.4 copy-start.1
  128.9 21.7 %all-to-all-start.1 = ((bf16[16,32,512]{2,1,0:T(8,128)(2,1)}), bf16[16,32,512]{2,1,0:T(8,128)(2,1)}, u32[]{:S(2)}, u32[]{:S(2)}) async-start(bf16[16,32,512]{2,1,0:T(8,128)(2,1)} %bitcast.120), calls=%async_computation.1 | async-start | bytes 1048576 | tf_op jit(solution)/shard_map/all_to_all | solution.py:94
  133.2 182.3 %all-reduce.10.cloned.1.call-start = ((), (), s32[]{:S(2)}) async-start(), calls=%async_computation.4 | async-start | bytes 5242880 | tf_op jit(solution)/shard_map/psum | solution.py:108
  156.1 280.8 %all-reduce.8.cloned.1.call-start = ((), (), s32[]{:S(2)}) async-start(), calls=%async_computation.3 | async-start | bytes 2097152 | tf_op jit(solution)/shard_map/psum | solution.py:109
  436.9 2.3 copy-start.4
Sparse Core Ops, SparseCore 0:
  10.1 84.9 all-gather.1
  156.2 159.2 all-reduce.9
  317.8 119.0 all-reduce.7
